TPU v7x, 32 devices: a whole 2x2x4 slice. The times are simulated.
32 devices in a mesh: inst: 2 (over y), cell: 16 (over z, x, core).
Axes of the slice: x: 2, y: 2, z: 4, core: 2. Of those that a mesh axis runs over, the one named last changes fastest.
Arguments:
- adjoint: bfloat16 [4, 5, 32, 16, 256], P('inst', None, 'cell'), may hold values from -6 to 6
- flux_jac: bfloat16 [4, 5, 3, 32, 16, 256], P('inst', None, None, 'cell'), may hold values from -1.25 to 1.25
- shift: float32 [32, 16, 256], P('cell', 'inst'), may hold values from 0.1 to 2
Outputs:
- mesh_adjoint: float32 [3, 32, 16, 256], P(None, 'cell', 'inst')
- residual: float32 [3, 32, 16, 256], P(None, 'cell', 'inst')
All inputs are finite; a program needn't handle non-finite values.
Results may differ from a plain program's by a relative error of at most 0.0003.
Values may be sent and summed in bfloat16 or wider, within the bound.
A program may use at most 64 MiB of HBM per device.

v0:
```python
import jax
import jax.numpy as jnp
from jax import lax
from jax.sharding import PartitionSpec as P

ITERS = 3


mu_shear = 1.0
lame_first = 1.5


def padded_2(block, sides, width):
    for axis, dim in sides:
        count = lax.axis_size(axis)
        forward = [(i, i + 1) for i in range(count - 1)]
        backward = [(target, source) for source, target in forward]
        low = lax.ppermute(
            lax.slice_in_dim(block, block.shape[dim] - width, None, axis=dim), axis, forward
        )
        high = lax.ppermute(lax.slice_in_dim(block, 0, width, axis=dim), axis, backward)
        block = jnp.concatenate([low, block, high], axis=dim)
    return block


def operate(field, shift):
    padded = padded_2(field, (("inst", 2), ("cell", 1)), 1)
    padded = jnp.pad(padded, ((0, 0), (0, 0), (0, 0), (1, 1)))
    center = padded[:, 1:-1, 1:-1, 1:-1]
    beside = padded[:, 2:, 1:-1, 1:-1] + padded[:, :-2, 1:-1, 1:-1]
    beside = beside + padded[:, 1:-1, 2:, 1:-1] + padded[:, 1:-1, :-2, 1:-1]
    beside = beside + padded[:, 1:-1, 1:-1, 2:] + padded[:, 1:-1, 1:-1, :-2]
    corner = padded[:, :-1, :-1, :-1]
    diverge = (
        padded[0, 1:, :-1, :-1]
        - corner[0]
        + (padded[1, :-1, 1:, :-1] - corner[1])
        + (padded[2, :-1, :-1, 1:] - corner[2])
    )
    cell_first = lax.axis_index("cell") == 0
    inst_first = lax.axis_index("inst") == 0
    keep_rows = jnp.where((jnp.arange(diverge.shape[0]) == 0) & cell_first, 0.0, 1.0).astype(
        jnp.float32
    )
    keep_cols = jnp.where((jnp.arange(diverge.shape[1]) == 0) & inst_first, 0.0, 1.0).astype(
        jnp.float32
    )
    keep_depth = jnp.where(jnp.arange(diverge.shape[2]) == 0, 0.0, 1.0).astype(jnp.float32)
    diverge = (
        diverge * keep_rows[:, None, None] * keep_cols[None, :, None] * keep_depth[None, None, :]
    )
    inner = diverge[1:, 1:, 1:]
    grad_part = jnp.stack(
        [diverge[:-1, 1:, 1:] - inner, diverge[1:, :-1, 1:] - inner, diverge[1:, 1:, :-1] - inner]
    )
    return mu_shear * (6.0 * center - beside) + shift * center + lame_first * grad_part


def two_products(residual, image):
    return lax.psum((jnp.sum(residual * residual), jnp.sum(residual * image)), ("inst", "cell"))


def local(adjoint, flux_jac, shift):
    padded = padded_2(adjoint, (("cell", 2),), 1)
    upper = jnp.einsum(
        "ivkxyz,ivxyz->kxyz", flux_jac, padded[:, :, 2:], preferred_element_type=jnp.float32
    )
    lower = jnp.einsum(
        "ivkxyz,ivxyz->kxyz", flux_jac, padded[:, :, :-2], preferred_element_type=jnp.float32
    )
    partial_sum = upper - lower
    block_cols = shift.shape[1]
    totals = lax.psum(partial_sum, "inst")
    sens = lax.dynamic_slice_in_dim(totals, lax.axis_index("inst") * block_cols, block_cols, 2)
    mesh_adjoint = jnp.zeros_like(sens)
    residual = sens
    image = operate(residual, shift)
    norm_now, product = two_products(residual, image)
    alpha = norm_now / product
    direction, along = (residual, image)
    for sweep in range(ITERS):
        mesh_adjoint = mesh_adjoint + alpha * direction
        residual = residual - alpha * along
        if sweep + 1 < ITERS:
            image = operate(residual, shift)
            norm_next, product = two_products(residual, image)
            ratio = norm_next / norm_now
            alpha = norm_next / (product - ratio * norm_next / alpha)
            direction = residual + ratio * direction
            along = image + ratio * along
            norm_now = norm_next
    return (mesh_adjoint, residual)


def solution(mesh):
    placed = (
        P("inst", None, "cell", None, None),
        P("inst", None, None, "cell", None, None),
        P("cell", "inst", None),
    )
    return jax.shard_map(
        local,
        mesh=mesh,
        in_specs=placed,
        out_specs=(P(None, "cell", "inst", None), P(None, "cell", "inst", None)),
        check_vma=False,
    )
```

profile of v0, /device:TPU:0, one launch (start us, length us, event | category | flops | bytes accessed | tf_op | source)
XLA Modules:
  0.0 234.0 jit_solution(14785577434391238408)
XLA Ops:
  7.2 1.0 fusion.56
  8.2 1.3 collective-permute-start
  9.5 3.0 %collective-permute-start.1 = (bf16[2,5,1,16,256]{4,3,2,1,0:T(8,128)(2,1)S(1)}, bf16[2,5,1,16,256]{4,3,2,1,0:T(8,128)(2,1)S(1)}, u32[]{:S(2)}, u32[]{:S(2)}) collective-permute-start(bf16[2,5,1,16,256]{4,3,2,1,0:T(8,128)(2,1)S(1)} %get-tuple-element.22), channel_id=1, source_target_pairs={{0,1},{1,2},{2,3},{3,4},{4,5},{5,6},{6,7},{7,8},{8,9},{9,10},{10,1... | collective-permute-start | bytes 245768 | tf_op jit(solution)/shard_map/ppermute | solution.py:18
  12.6 0.9 collective-permute-done.1
  14.5 27.2 %all-reduce.8.cloned.1.call-done = f32[3,2,16,256]{3,2,1,0:T(8,128)} async-done(((f32[3,2,16,256]{3,2,1,0:T(8,128)}), f32[3,2,16,256]{3,2,1,0:T(8,128)}) %all-reduce.8.cloned.1.call-update) | async-done | bytes 98320 | tf_op jit(solution)/shard_map/psum | solution.py:73
  41.6 0.9 constant_dynamic-slice_fusion.1
  42.5 2.1 collective-permute-start.2
  44.6 1.3 collective-permute-start.3
  45.9 0.8 constant_dynamic-slice_fusion.2
  46.7 3.4 %collective-permute-done.3 = f32[3,2,1,256]{3,2,1,0:T(1,128)S(1)} collective-permute-done((f32[3,2,1,256]{3,2,1,0:T(1,128)S(1)}, f32[3,2,1,256]{3,2,1,0:T(1,128)S(1)}, u32[]{:S(2)}, u32[]{:S(2)}) %collective-permute-start.3) | collective-permute-done | bytes 6176 | tf_op jit(solution)/shard_map/ppermute | solution.py:21
  50.2 1.3 collective-permute-start.4
  51.5 3.0 %collective-permute-start.5 = (f32[3,1,10,256]{3,2,1,0:T(8,128)S(1)}, f32[3,1,10,256]{3,2,1,0:T(8,128)S(1)}, u32[]{:S(2)}, u32[]{:S(2)}) collective-permute-start(f32[3,1,10,256]{3,2,1,0:T(8,128)S(1)} %get-tuple-element.27), channel_id=1, source_target_pairs={{0,1},{1,2},{2,3},{3,4},{4,5},{5,6},{6,7},{7,8},{8,9},{9,10},{10,1... | collective-permute-start | bytes 92168 | tf_op jit(solution)/shard_map/ppermute | solution.py:18
  54.5 0.8 collective-permute-done.5
  56.4 0.7 multiply_reduce_fusion.4
  57.1 43.0 %all-reduce.5 = (f32[]{:T(128)}, f32[]{:T(128)}) all-reduce(f32[]{:T(128)} %get-tuple-element.9, f32[]{:T(128)} %get-tuple-element.8), channel_id=1, replica_groups=mesh['inst'=2,'cell'=16] {'inst','cell'}, use_global_device_ids=true, to_apply=%region_2.3 | all-reduce | flops 2 | bytes 16 | tf_op jit(solution)/shard_map/psum | solution.py:60
  101.4 4.4 %collective-permute-start.6 = (f32[3,2,1,256]{3,2,1,0:T(1,128)S(1)}, f32[3,2,1,256]{3,2,1,0:T(1,128)S(1)}, u32[]{:S(2)}, u32[]{:S(2)}) collective-permute-start(f32[3,2,1,256]{3,2,1,0:T(1,128)S(1)} %get-tuple-element.44), channel_id=1, source_target_pairs={{0,16},{1,17},{2,18},{3,19},{4,20},{5,21},{6,22},{7,23},{8,24},{9,... | collective-permute-start | bytes 18440 | tf_op jit(solution)/shard_map/ppermute | solution.py:18
  105.8 1.3 collective-permute-start.7
  107.1 4.2 %collective-permute-done.7 = f32[3,2,1,256]{3,2,1,0:T(1,128)S(1)} collective-permute-done((f32[3,2,1,256]{3,2,1,0:T(1,128)S(1)}, f32[3,2,1,256]{3,2,1,0:T(1,128)S(1)}, u32[]{:S(2)}, u32[]{:S(2)}) %collective-permute-start.7) | collective-permute-done | bytes 6176 | tf_op jit(solution)/shard_map/ppermute | solution.py:21
  111.4 1.3 collective-permute-start.8
  112.7 3.0 %collective-permute-start.9 = (f32[3,1,10,256]{3,2,1,0:T(8,128)S(1)}, f32[3,1,10,256]{3,2,1,0:T(8,128)S(1)}, u32[]{:S(2)}, u32[]{:S(2)}) collective-permute-start(f32[3,1,10,256]{3,2,1,0:T(8,128)S(1)} %get-tuple-element.25), channel_id=1, source_target_pairs={{0,1},{1,2},{2,3},{3,4},{4,5},{5,6},{6,7},{7,8},{8,9},{9,10},{10,1... | collective-permute-start | bytes 92168 | tf_op jit(solution)/shard_map/ppermute | solution.py:18
  115.7 0.9 collective-permute-done.9
  117.0 0.7 multiply_reduce_fusion.2
  117.7 42.4 %all-reduce.4 = (f32[]{:T(128)}, f32[]{:T(128)}) all-reduce(f32[]{:T(128)} %get-tuple-element.7, f32[]{:T(128)} %get-tuple-element.6), channel_id=1, replica_groups=mesh['inst'=2,'cell'=16] {'inst','cell'}, use_global_device_ids=true, to_apply=%region_6.7 | all-reduce | flops 2 | bytes 16 | tf_op jit(solution)/shard_map/psum | solution.py:60
  164.7 4.4 %collective-permute-start.10 = (f32[3,2,1,256]{3,2,1,0:T(1,128)S(1)}, f32[3,2,1,256]{3,2,1,0:T(1,128)S(1)}, u32[]{:S(2)}, u32[]{:S(2)}) collective-permute-start(f32[3,2,1,256]{3,2,1,0:T(1,128)S(1)} %get-tuple-element.42), channel_id=1, source_target_pairs={{0,16},{1,17},{2,18},{3,19},{4,20},{5,21},{6,22},{7,23},{8,24},{9,... | collective-permute-start | bytes 18440 | tf_op jit(solution)/shard_map/ppermute | solution.py:18
  169.2 1.3 collective-permute-start.11
  170.5 4.2 %collective-permute-done.11 = f32[3,2,1,256]{3,2,1,0:T(1,128)S(1)} collective-permute-done((f32[3,2,1,256]{3,2,1,0:T(1,128)S(1)}, f32[3,2,1,256]{3,2,1,0:T(1,128)S(1)}, u32[]{:S(2)}, u32[]{:S(2)}) %collective-permute-start.11) | collective-permute-done | bytes 6176 | tf_op jit(solution)/shard_map/ppermute | solution.py:21
  174.8 1.3 collective-permute-start.12
  176.1 3.0 %collective-permute-start.13 = (f32[3,1,10,256]{3,2,1,0:T(8,128)S(1)}, f32[3,1,10,256]{3,2,1,0:T(8,128)S(1)}, u32[]{:S(2)}, u32[]{:S(2)}) collective-permute-start(f32[3,1,10,256]{3,2,1,0:T(8,128)S(1)} %get-tuple-element.23), channel_id=1, source_target_pairs={{0,1},{1,2},{2,3},{3,4},{4,5},{5,6},{6,7},{7,8},{8,9},{9,10},{10,1... | collective-permute-start | bytes 92168 | tf_op jit(solution)/shard_map/ppermute | solution.py:18
  179.1 0.9 collective-permute-done.13
  180.3 0.7 multiply_reduce_fusion
  181.0 41.4 %all-reduce.3 = (f32[]{:T(128)}, f32[]{:T(128)}) all-reduce(f32[]{:T(128)} %get-tuple-element.5, f32[]{:T(128)} %get-tuple-element.4), channel_id=1, replica_groups=mesh['inst'=2,'cell'=16] {'inst','cell'}, use_global_device_ids=true, to_apply=%region_10.11 | all-reduce | flops 2 | bytes 16 | tf_op jit(solution)/shard_map/psum | solution.py:60
  226.5 0.7 multiply_subtract_fusion
  (42 shorter events, 3.0 us)
Async XLA Ops:
  7.2 6.3 %copy-start = (bf16[2,5,2,16,256]{4,3,2,1,0:T(8,128)(2,1)S(1)}, bf16[2,5,2,16,256]{4,3,2,1,0:T(8,128)(2,1)}, u32[]{:S(2)}) copy-start(bf16[2,5,2,16,256]{4,3,2,1,0:T(8,128)(2,1)} %param.3) | copy-start | bytes 491524
  7.2 34.5 %all-reduce.8.cloned.1.call-start = ((), (), s32[]{:S(2)}) async-start(), calls=%async_computation | async-start | bytes 196608 | tf_op jit(solution)/shard_map/psum | solution.py:73
  8.2 4.4 %collective-permute-start = (bf16[2,5,1,16,256]{4,3,2,1,0:T(8,128)(2,1)S(1)}, bf16[2,5,1,16,256]{4,3,2,1,0:T(8,128)(2,1)S(1)}, u32[]{:S(2)}, u32[]{:S(2)}) collective-permute-start(bf16[2,5,1,16,256]{4,3,2,1,0:T(8,128)(2,1)S(1)} %get-tuple-element.21), channel_id=1, source_target_pairs={{1,0},{2,1},{3,2},{4,3},{5,4},{6,5},{7,6},{8,7},{9,8},{10,9},{11,1... | collective-permute-start | bytes 245768 | tf_op jit(solution)/shard_map/ppermute | solution.py:21
  9.5 3.9 %collective-permute-start.1 = (bf16[2,5,1,16,256]{4,3,2,1,0:T(8,128)(2,1)S(1)}, bf16[2,5,1,16,256]{4,3,2,1,0:T(8,128)(2,1)S(1)}, u32[]{:S(2)}, u32[]{:S(2)}) collective-permute-start(bf16[2,5,1,16,256]{4,3,2,1,0:T(8,128)(2,1)S(1)} %get-tuple-element.22), channel_id=1, source_target_pairs={{0,1},{1,2},{2,3},{3,4},{4,5},{5,6},{6,7},{7,8},{8,9},{9,10},{10,1... | collective-permute-start | bytes 245768 | tf_op jit(solution)/shard_map/ppermute | solution.py:18
  12.6 1.0 copy-start.1
  42.5 4.2 %collective-permute-start.2 = (f32[3,2,1,256]{3,2,1,0:T(1,128)S(1)}, f32[3,2,1,256]{3,2,1,0:T(1,128)S(1)}, u32[]{:S(2)}, u32[]{:S(2)}) collective-permute-start(f32[3,2,1,256]{3,2,1,0:T(1,128)S(1)} %get-tuple-element.29), channel_id=1, source_target_pairs={{0,16},{1,17},{2,18},{3,19},{4,20},{5,21},{6,22},{7,23},{8,24},{9,... | collective-permute-start | bytes 18440 | tf_op jit(solution)/shard_map/ppermute | solution.py:18
  44.6 5.5 %collective-permute-start.3 = (f32[3,2,1,256]{3,2,1,0:T(1,128)S(1)}, f32[3,2,1,256]{3,2,1,0:T(1,128)S(1)}, u32[]{:S(2)}, u32[]{:S(2)}) collective-permute-start(f32[3,2,1,256]{3,2,1,0:T(1,128)S(1)} %get-tuple-element.30), channel_id=1, source_target_pairs={{16,0},{17,1},{18,2},{19,3},{20,4},{21,5},{22,6},{23,7},{24,8},{25... | collective-permute-start | bytes 18440 | tf_op jit(solution)/shard_map/ppermute | solution.py:21
  50.2 4.4 %collective-permute-start.4 = (f32[3,1,10,256]{3,2,1,0:T(8,128)S(1)}, f32[3,1,10,256]{3,2,1,0:T(8,128)S(1)}, u32[]{:S(2)}, u32[]{:S(2)}) collective-permute-start(f32[3,1,10,256]{3,2,1,0:T(8,128)S(1)} %get-tuple-element.28), channel_id=1, source_target_pairs={{1,0},{2,1},{3,2},{4,3},{5,4},{6,5},{7,6},{8,7},{9,8},{10,9},{11,1... | collective-permute-start | bytes 92168 | tf_op jit(solution)/shard_map/ppermute | solution.py:21
  51.5 3.9 %collective-permute-start.5 = (f32[3,1,10,256]{3,2,1,0:T(8,128)S(1)}, f32[3,1,10,256]{3,2,1,0:T(8,128)S(1)}, u32[]{:S(2)}, u32[]{:S(2)}) collective-permute-start(f32[3,1,10,256]{3,2,1,0:T(8,128)S(1)} %get-tuple-element.27), channel_id=1, source_target_pairs={{0,1},{1,2},{2,3},{3,4},{4,5},{5,6},{6,7},{7,8},{8,9},{9,10},{10,1... | collective-permute-start | bytes 92168 | tf_op jit(solution)/shard_map/ppermute | solution.py:18
  55.7 0.7 copy-start.3
  56.4 45.0 %copy-start.2 = (f32[3,2,16,256]{3,2,1,0:T(8,128)S(1)}, f32[3,2,16,256]{3,2,1,0:T(8,128)}, u32[]{:S(2)}) copy-start(f32[3,2,16,256]{3,2,1,0:T(8,128)} %all-reduce.8.cloned.1.call-done) | copy-start | bytes 294916
  101.4 5.7 %collective-permute-start.6 = (f32[3,2,1,256]{3,2,1,0:T(1,128)S(1)}, f32[3,2,1,256]{3,2,1,0:T(1,128)S(1)}, u32[]{:S(2)}, u32[]{:S(2)}) collective-permute-start(f32[3,2,1,256]{3,2,1,0:T(1,128)S(1)} %get-tuple-element.44), channel_id=1, source_target_pairs={{0,16},{1,17},{2,18},{3,19},{4,20},{5,21},{6,22},{7,23},{8,24},{9,... | collective-permute-start | bytes 18440 | tf_op jit(solution)/shard_map/ppermute | solution.py:18
  105.8 5.5 %collective-permute-start.7 = (f32[3,2,1,256]{3,2,1,0:T(1,128)S(1)}, f32[3,2,1,256]{3,2,1,0:T(1,128)S(1)}, u32[]{:S(2)}, u32[]{:S(2)}) collective-permute-start(f32[3,2,1,256]{3,2,1,0:T(1,128)S(1)} %get-tuple-element.45), channel_id=1, source_target_pairs={{16,0},{17,1},{18,2},{19,3},{20,4},{21,5},{22,6},{23,7},{24,8},{25... | collective-permute-start | bytes 18440 | tf_op jit(solution)/shard_map/ppermute | solution.py:21
  111.4 4.3 %collective-permute-start.8 = (f32[3,1,10,256]{3,2,1,0:T(8,128)S(1)}, f32[3,1,10,256]{3,2,1,0:T(8,128)S(1)}, u32[]{:S(2)}, u32[]{:S(2)}) collective-permute-start(f32[3,1,10,256]{3,2,1,0:T(8,128)S(1)} %get-tuple-element.26), channel_id=1, source_target_pairs={{1,0},{2,1},{3,2},{4,3},{5,4},{6,5},{7,6},{8,7},{9,8},{10,9},{11,1... | collective-permute-start | bytes 92168 | tf_op jit(solution)/shard_map/ppermute | solution.py:21
  112.7 3.9 %collective-permute-start.9 = (f32[3,1,10,256]{3,2,1,0:T(8,128)S(1)}, f32[3,1,10,256]{3,2,1,0:T(8,128)S(1)}, u32[]{:S(2)}, u32[]{:S(2)}) collective-permute-start(f32[3,1,10,256]{3,2,1,0:T(8,128)S(1)} %get-tuple-element.25), channel_id=1, source_target_pairs={{0,1},{1,2},{2,3},{3,4},{4,5},{5,6},{6,7},{7,8},{8,9},{9,10},{10,1... | collective-permute-start | bytes 92168 | tf_op jit(solution)/shard_map/ppermute | solution.py:18
  164.7 5.8 %collective-permute-start.10 = (f32[3,2,1,256]{3,2,1,0:T(1,128)S(1)}, f32[3,2,1,256]{3,2,1,0:T(1,128)S(1)}, u32[]{:S(2)}, u32[]{:S(2)}) collective-permute-start(f32[3,2,1,256]{3,2,1,0:T(1,128)S(1)} %get-tuple-element.42), channel_id=1, source_target_pairs={{0,16},{1,17},{2,18},{3,19},{4,20},{5,21},{6,22},{7,23},{8,24},{9,... | collective-permute-start | bytes 18440 | tf_op jit(solution)/shard_map/ppermute | solution.py:18
  169.2 5.5 %collective-permute-start.11 = (f32[3,2,1,256]{3,2,1,0:T(1,128)S(1)}, f32[3,2,1,256]{3,2,1,0:T(1,128)S(1)}, u32[]{:S(2)}, u32[]{:S(2)}) collective-permute-start(f32[3,2,1,256]{3,2,1,0:T(1,128)S(1)} %get-tuple-element.43), channel_id=1, source_target_pairs={{16,0},{17,1},{18,2},{19,3},{20,4},{21,5},{22,6},{23,7},{24,8},{25... | collective-permute-start | bytes 18440 | tf_op jit(solution)/shard_map/ppermute | solution.py:21
  174.8 4.3 %collective-permute-start.12 = (f32[3,1,10,256]{3,2,1,0:T(8,128)S(1)}, f32[3,1,10,256]{3,2,1,0:T(8,128)S(1)}, u32[]{:S(2)}, u32[]{:S(2)}) collective-permute-start(f32[3,1,10,256]{3,2,1,0:T(8,128)S(1)} %get-tuple-element.24), channel_id=1, source_target_pairs={{1,0},{2,1},{3,2},{4,3},{5,4},{6,5},{7,6},{8,7},{9,8},{10,9},{11,1... | collective-permute-start | bytes 92168 | tf_op jit(solution)/shard_map/ppermute | solution.py:21
  176.1 3.9 %collective-permute-start.13 = (f32[3,1,10,256]{3,2,1,0:T(8,128)S(1)}, f32[3,1,10,256]{3,2,1,0:T(8,128)S(1)}, u32[]{:S(2)}, u32[]{:S(2)}) collective-permute-start(f32[3,1,10,256]{3,2,1,0:T(8,128)S(1)} %get-tuple-element.23), channel_id=1, source_target_pairs={{0,1},{1,2},{2,3},{3,4},{4,5},{5,6},{6,7},{7,8},{8,9},{9,10},{10,1... | collective-permute-start | bytes 92168 | tf_op jit(solution)/shard_map/ppermute | solution.py:18
Sparse Core Ops, SparseCore 0:
  14.6 27.0 all-reduce.7
where the time goes:
time: 235 us; the launch traced here: 234 us
  blocking collectives  127 us (54%)
  waiting for transfers between devices  42.5 us (18%)
  starting transfers between devices  32.1 us (14%)
  between operations  24.4 us (10%)
  other arithmetic  4.82 us (2%)
  local copies, waits for them, and re-layouts  3.46 us (1%)
    psum x3, blocking collectives, two_products(): lax.psum((jnp.sum(residual * residual), jnp.sum(residual * image)), ('ins...  127 us
    psum x1, waiting for transfers between devices, local(): totals = lax.psum(partial_sum, 'inst')  27.2 us
    ppermute x7, starting transfers between devices, padded_2(): lax.ppermute(lax.slice_in_dim(block, block.shape[dim] - width, None, axis...  23 us
    ppermute x7, waiting for transfers between devices, padded_2(): lax.ppermute(lax.slice_in_dim(block, 0, width, axis=dim), axis, backward)  11.8 us
    ppermute x7, starting transfers between devices, padded_2(): lax.ppermute(lax.slice_in_dim(block, 0, width, axis=dim), axis, backward)  9.04 us
  transfers between devices with their start and end apart: 15, of which 8 were waited for; matrix products, arithmetic and copies ran while one was open for 0% of the time, Pallas kernels for 0%

commit v1 on v0

v1 whole, which is shorter than its diff:
```python
import functools

import jax
import jax.numpy as jnp
from jax import lax
from jax.experimental import pallas as pl
from jax.experimental.pallas import tpu as pltpu
from jax.sharding import PartitionSpec as P

ITERS = 3
LAME = 1.5
CENTER = 10.0
SPREAD = 8.0
HALO = 3
MESH = pl.DeviceIdType.MESH
F32 = jnp.float32


def remote(src, dst, send_sem, recv_sem, device):
    return pltpu.make_async_remote_copy(
        src_ref=src,
        dst_ref=dst,
        send_sem=send_sem,
        recv_sem=recv_sem,
        device_id=device,
        device_id_type=MESH,
    )


def apply_operator(src, dst, sh, lo, hi, valid_row, edges):
    y_first, y_last, z_first, z_last = edges
    wy, nz = src.shape[2], src.shape[3]

    def up_y(v):
        return jnp.where(y_last, 0.0, pltpu.roll(v, wy - 1, 0))

    def down_y(v):
        return jnp.where(y_first, 0.0, pltpu.roll(v, 1, 0))

    def up_z(v):
        return jnp.where(z_last, 0.0, pltpu.roll(v, nz - 1, 1))

    def down_z(v):
        return jnp.where(z_first, 0.0, pltpu.roll(v, 1, 1))

    before = None
    for row in range(lo - 1, hi + 1):
        fields = [src[k, row] for k in range(3)]
        uy, uz = up_y(fields[1]), up_z(fields[2])
        dv = (src[0, row + 1] - fields[0]) + (uy - fields[1]) + (uz - fields[2])
        dv = jnp.where(valid_row(row), dv, 0.0)
        if row >= lo:
            diag = sh[row - 1] + (6.0 - CENTER)
            shifted = [before, down_y(dv), down_z(dv)]
            for k in range(3):
                u = fields[k]
                beside = src[k, row - 1] + src[k, row + 1]
                beside = beside + (uy if k == 1 else up_y(u)) + down_y(u)
                beside = beside + (uz if k == 2 else up_z(u)) + down_z(u)
                out = (diag * u - beside + LAME * (shifted[k] - dv)) * (1.0 / SPREAD)
                dst[k, row] = jnp.where(valid_row(row), out, 0.0)
        before = dv


def coefficients(mu):
    def inner(a, b, skip=0):
        total = None
        for p, x in enumerate(a):
            for q, y in enumerate(b):
                if x is None or y is None:
                    continue
                term = x * y * mu[p + q]
                total = term if total is None else total + term
        return total

    def times(a):
        return [
            (CENTER * a[j] if j < len(a) else 0.0) + (SPREAD * a[j - 1] if j > 0 else 0.0)
            for j in range(len(a) + 1)
        ]

    one = jnp.ones_like(mu[0])
    solution_at, residual, direction = [], [one], [one]
    norm_now = mu[0]
    for sweep in range(ITERS):
        image = times(direction)
        alpha = norm_now / inner(direction, image)
        solution_at = [
            (solution_at[j] if j < len(solution_at) else 0.0) + alpha * direction[j]
            for j in range(len(direction))
        ]
        residual = [
            (residual[j] if j < len(residual) else 0.0) - alpha * image[j]
            for j in range(len(image))
        ]
        if sweep + 1 < ITERS:
            norm_next = inner(residual, residual)
            ratio = norm_next / norm_now
            direction = [
                residual[j] + (ratio * direction[j] if j < len(direction) else 0.0)
                for j in range(len(residual))
            ]
            norm_now = norm_next
    return solution_at, residual


def kernel(
    n_inst, n_cell, cols, window,
    adj_hbm, flux_hbm, shift_hbm, x_ref, r_ref,
    adj, flux, halo, part, got, u0, u1, u2, u3, sh, row_out, gath, gath2,
    load_sem, halo_send, halo_recv, sh_send, sh_recv, y_send, y_recv,
    x_send, x_recv, g_send, g_recv, h_send, h_recv,
):
    i, c = lax.axis_index("inst"), lax.axis_index("cell")
    wy = window * cols
    nv = adj.shape[0] * adj.shape[1]
    nz = adj.shape[-1]

    def start_of(j):
        return jnp.clip(j - 1, 0, n_inst - window)

    own_at = pl.multiple_of((i - start_of(i)) * cols, cols)

    loads = [
        pltpu.make_async_copy(adj_hbm, adj, load_sem.at[0]),
        pltpu.make_async_copy(flux_hbm, flux, load_sem.at[1]),
        pltpu.make_async_copy(shift_hbm, sh.at[pl.ds(2, 2), pl.ds(own_at, cols)], load_sem.at[2]),
    ]
    for load in loads:
        load.start()

    barrier = pltpu.get_barrier_semaphore()
    for d in range(1, n_cell):
        pl.semaphore_signal(barrier, inc=1, device_id=(i, lax.rem(c + d, n_cell)), device_id_type=MESH)
    for d in range(1, n_inst):
        pl.semaphore_signal(barrier, inc=1, device_id=(lax.rem(i + d, n_inst), c), device_id_type=MESH)
    expected = n_cell - 1 + n_inst - 1
    for dj in range(-(window - 1), window):
        if dj == 0:
            continue
        for dc in (-1, 1):
            there = (i + dj >= 0) & (i + dj < n_inst) & (c + dc >= 0) & (c + dc < n_cell)
            expected = expected + jnp.where(there, 1, 0)

            @pl.when(there)
            def _():
                pl.semaphore_signal(barrier, inc=1, device_id=(i + dj, c + dc), device_id_type=MESH)

    pl.semaphore_wait(barrier, expected)

    def halo_copy(dc):
        side = 0 if dc == 1 else 1
        return remote(
            adj_hbm.at[:, :, 1 if dc == 1 else 0], halo.at[side],
            halo_send.at[side], halo_recv.at[side], (i, c + dc),
        )

    def inside(dc):
        return (c + dc >= 0) & (c + dc < n_cell)

    for dc in (1, -1):
        @pl.when(inside(dc))
        def _():
            halo_copy(dc).start()

    def sh_copy(dj, dc):
        j = i + dj
        slot = jnp.clip(i - start_of(j), 0, window - 1)
        at = pl.multiple_of(slot * cols, cols)
        return remote(
            shift_hbm, sh.at[pl.ds(2 - 2 * dc, 2), pl.ds(at, cols)],
            sh_send.at[dj + window - 1, dc + 1], sh_recv.at[slot, dc + 1], (j, c + dc),
        )

    def sh_valid(dj, dc):
        j = i + dj
        first = start_of(j)
        return (j >= 0) & (j < n_inst) & inside(dc) & (i >= first) & (i < first + window)

    sh_moves = [
        (dj, dc)
        for dj in range(-(window - 1), window)
        for dc in (-1, 0, 1)
        if (dj, dc) != (0, 0)
    ]
    for dj, dc in sh_moves:
        @pl.when(sh_valid(dj, dc))
        def _():
            sh_copy(dj, dc).start()

    @pl.when(c == 0)
    def _():
        halo[0] = jnp.zeros_like(halo[0])
        sh[0:2] = jnp.zeros_like(sh[0:2])
        u0[:, 0:3] = jnp.zeros_like(u0[:, 0:3])

    @pl.when(c == 1)
    def _():
        u0[:, 0:1] = jnp.zeros_like(u0[:, 0:1])

    @pl.when(c == n_cell - 1)
    def _():
        halo[1] = jnp.zeros_like(halo[1])
        sh[4:6] = jnp.zeros_like(sh[4:6])
        u0[:, 5:8] = jnp.zeros_like(u0[:, 5:8])

    @pl.when(c == n_cell - 2)
    def _():
        u0[:, 7:8] = jnp.zeros_like(u0[:, 7:8])

    loads[0].wait()
    loads[1].wait()

    n_v = adj.shape[1]

    def own_terms(k):
        for y0 in range(0, adj.shape[3], 16):
            ys = slice(y0, y0 + 16)
            low, high = None, None
            for v in range(nv):
                a, b = v // n_v, v % n_v
                t0 = flux[a, b, k, 0, ys].astype(F32) * adj[a, b, 1, ys].astype(F32)
                t1 = flux[a, b, k, 1, ys].astype(F32) * adj[a, b, 0, ys].astype(F32)
                low = t0 if low is None else low + t0
                high = t1 if high is None else high + t1
            part[k, 0, ys] = low
            part[k, 1, ys] = -high

    def halo_terms(k):
        for y0 in range(0, adj.shape[3], 16):
            ys = slice(y0, y0 + 16)
            low, high = part[k, 0, ys], part[k, 1, ys]
            for v in range(nv):
                a, b = v // n_v, v % n_v
                low = low - flux[a, b, k, 0, ys].astype(F32) * halo[0, a, b, ys].astype(F32)
                high = high + flux[a, b, k, 1, ys].astype(F32) * halo[1, a, b, ys].astype(F32)
            part[k, 0, ys] = low
            part[k, 1, ys] = high

    for k in range(3):
        own_terms(k)

    for dc in (1, -1):
        @pl.when(inside(-dc))
        def _():
            halo_copy(dc).wait_recv()

    def y_copy(k, d):
        j = lax.rem(i + d, n_inst)
        at = pl.multiple_of(start_of(j) * cols, cols)
        return remote(
            part.at[k, :, pl.ds(at, wy)], got.at[d - 1, k],
            y_send.at[d - 1, k], y_recv.at[d - 1, k], (j, c),
        )

    for k in range(3):
        halo_terms(k)
        for d in range(1, n_inst):
            y_copy(k, d).start()

    x_moves = {1: (3, 1, 2), -1: (3, 5, 2), 2: (4, 0, 1), -2: (3, 7, 1)}

    def x_copy(k, dc):
        src, dst, rows = x_moves[dc]
        slot = sorted(x_moves).index(dc)
        return remote(
            u0.at[k, pl.ds(src, rows)], u0.at[k, pl.ds(dst, rows)],
            x_send.at[slot, k], x_recv.at[slot, k], (i, c + dc),
        )

    my_at = pl.multiple_of(start_of(i) * cols, cols)
    for k in range(3):
        for d in range(1, n_inst):
            y_copy(k, d).wait_recv()
        total = part[k, :, pl.ds(my_at, wy)]
        for d in range(1, n_inst):
            total = total + got[d - 1, k]
        u0[k, 3:5] = total
        for dc in x_moves:
            @pl.when(inside(dc))
            def _():
                x_copy(k, dc).start()

    loads[2].wait()
    for dj, dc in sh_moves:
        @pl.when(sh_valid(dj, dc))
        def _():
            sh_copy(dj, dc).wait_send()
    for slot in range(window):
        for dc in (-1, 0, 1):
            owner = start_of(i) + slot
            there = inside(-dc)
            if dc == 0:
                there = there & (owner != i)

            @pl.when(there)
            def _():
                at = slot * cols
                remote(
                    shift_hbm, sh.at[pl.ds(2 - 2 * dc, 2), pl.ds(at, cols)],
                    sh_send.at[0, 0], sh_recv.at[slot, dc + 1], (i, c),
                ).wait_recv()

    for k in range(3):
        for dc in x_moves:
            @pl.when(inside(-dc))
            def _():
                x_copy(k, dc).wait_recv()

    shape = (wy, nz)
    y_at = lax.broadcasted_iota(jnp.int32, shape, 0)
    z_at = lax.broadcasted_iota(jnp.int32, shape, 1)
    edges = (y_at == 0, y_at == wy - 1, z_at == 0, z_at == nz - 1)

    def valid_row(row):
        place = 2 * c + row - HALO
        return (place >= 0) & (place < 2 * n_cell)

    apply_operator(u0, u1, sh, 1, 6, valid_row, edges)
    apply_operator(u1, u2, sh, 2, 5, valid_row, edges)
    apply_operator(u2, u3, sh, 3, 4, valid_row, edges)

    basis = (u0, u1, u2, u3)
    lane = lax.broadcasted_iota(jnp.int32, (1, 128), 1)
    packed = jnp.zeros((1, 128), F32)
    for m in range(6):
        a, b = basis[m // 2], basis[(m + 1) // 2]
        total = None
        for k in range(3):
            for row in (3, 4):
                term = a[k, row] * b[k, row]
                total = term if total is None else total + term
        if window < n_inst:
            total = jnp.where((y_at >= own_at) & (y_at < own_at + cols), total, 0.0)
        value = jnp.sum(jnp.sum(total, axis=0, keepdims=True), axis=1, keepdims=True)
        packed = jnp.where(lane == m, value, packed)

    def gather_sum(packed, slot, buffer, send, recv, count, device):
        row_out[slot] = packed
        moves = [
            remote(row_out.at[slot], buffer.at[d - 1], send.at[d - 1], recv.at[d - 1], device(d))
            for d in range(1, count)
        ]
        for move in moves:
            move.start()
        total = packed
        for d, move in enumerate(moves):
            move.wait_recv()
            total = total + buffer[d]
        for move in moves:
            move.wait_send()
        return total

    packed = gather_sum(
        packed, 0, gath, g_send, g_recv, n_cell, lambda d: (i, lax.rem(c + d, n_cell))
    )
    if window < n_inst:
        packed = gather_sum(
            packed, 1, gath2, h_send, h_recv, n_inst, lambda d: (lax.rem(i + d, n_inst), c)
        )
    mu = [
        jnp.sum(jnp.where(lane == m, packed, 0.0), axis=1, keepdims=True) for m in range(6)
    ]
    at_x, at_r = coefficients(mu)

    own = pl.ds(own_at, cols)
    for k in range(3):
        for row in range(2):
            b = [basis[j][k, row + 3, own] for j in range(4)]
            x_ref[k, row] = at_x[0] * b[0] + at_x[1] * b[1] + at_x[2] * b[2]
            r_ref[k, row] = at_r[0] * b[0] + at_r[1] * b[1] + at_r[2] * b[2] + at_r[3] * b[3]

    for dc in (1, -1):
        @pl.when(inside(dc))
        def _():
            halo_copy(dc).wait_send()
    for k in range(3):
        for d in range(1, n_inst):
            y_copy(k, d).wait_send()
        for dc in x_moves:
            @pl.when(inside(dc))
            def _():
                x_copy(k, dc).wait_send()


def local(n_inst, n_cell, adjoint, flux_jac, shift):
    rows, cols, nz = shift.shape
    ny = adjoint.shape[3]
    window = min(3, n_inst)
    wy = window * cols
    field = pltpu.VMEM((3, rows + 2 * HALO, wy, nz), F32)
    dma = pltpu.SemaphoreType.DMA
    out = jax.ShapeDtypeStruct((3, rows, cols, nz), F32)
    peers = max(n_inst - 1, 1)
    return pl.pallas_call(
        functools.partial(kernel, n_inst, n_cell, cols, window),
        out_shape=(out, out),
        in_specs=[pl.BlockSpec(memory_space=pl.ANY)] * 3,
        out_specs=(pl.BlockSpec(memory_space=pltpu.VMEM),) * 2,
        scratch_shapes=[
            pltpu.VMEM(adjoint.shape, adjoint.dtype),
            pltpu.VMEM(flux_jac.shape, flux_jac.dtype),
            pltpu.VMEM((2,) + adjoint.shape[:2] + (ny, nz), adjoint.dtype),
            pltpu.VMEM((3, rows, ny, nz), F32),
            pltpu.VMEM((peers, 3, rows, wy, nz), F32),
            field, field, field, field,
            pltpu.VMEM((rows + 4, wy, nz), F32),
            pltpu.VMEM((2, 1, 128), F32),
            pltpu.VMEM((n_cell - 1, 1, 128), F32),
            pltpu.VMEM((peers, 1, 128), F32),
            dma((3,)),
            dma((2,)), dma((2,)),
            dma((2 * window - 1, 3)), dma((window, 3)),
            dma((peers, 3)), dma((peers, 3)),
            dma((4, 3)), dma((4, 3)),
            dma((n_cell - 1,)), dma((n_cell - 1,)),
            dma((peers,)), dma((peers,)),
        ],
        compiler_params=pltpu.CompilerParams(collective_id=0, has_side_effects=True),
    )(adjoint, flux_jac, shift)


def solution(mesh):
    placed = (
        P("inst", None, "cell", None, None),
        P("inst", None, None, "cell", None, None),
        P("cell", "inst", None),
    )
    return jax.shard_map(
        functools.partial(local, mesh.shape["inst"], mesh.shape["cell"]),
        mesh=mesh,
        in_specs=placed,
        out_specs=(P(None, "cell", "inst", None), P(None, "cell", "inst", None)),
        check_vma=False,
    )
```

time: 235 us -> 27.2 us (0.12)
  blocking collectives: 127 us -> 0 us
  waiting for transfers between devices: 42.5 us -> 0 us
  starting transfers between devices: 32.1 us -> 0 us
  Pallas kernels: 0 us -> 24.3 us
  between operations: 24.4 us -> 0.65 us
  other arithmetic: 4.82 us -> 0 us
    psum x3 -> x0, blocking collectives: 127 us -> none  [two_products(): lax.psum((jnp.sum(residual * residual), jnp.sum(residual * image)), ('ins...]
    ppermute x14 -> x0, starting transfers between devices: 32.1 us -> none  [the longest x7 23 us: padded_2(): lax.ppermute(lax.slice_in_dim(block, block.shape[dim] - width, None, axis...]
    psum x1 -> x0, waiting for transfers between devices: 27.2 us -> none  [local(): totals = lax.psum(partial_sum, 'inst')]
    pallas_call x0 -> x1, Pallas kernels: none -> 24.3 us  [local(): pl.pallas_call(functools.partial(kernel, n_inst, n_cell, cols, window), o...]
    ppermute x14 -> x0, waiting for transfers between devices: 15.3 us -> none  [the longest x7 11.8 us: padded_2(): lax.ppermute(lax.slice_in_dim(block, 0, width, axis=dim), axis, backward)]
  transfers between devices with their start and end apart: 15 -> 0, of which waited for: 8 -> 0; matrix products, arithmetic and copies ran while one was open for 0% -> 0% of each run, Pallas kernels for 0% -> 0%
where the time goes in v1:
time: 27.2 us; the launch traced here: 27 us
  Pallas kernels  24.3 us (89%)
  local copies, waits for them, and re-layouts  2.06 us (8%)
  between operations  0.65 us (2%)
    pallas_call x1, Pallas kernels, local(): pl.pallas_call(functools.partial(kernel, n_inst, n_cell, cols, window), o...  24.3 us
    unnamed x4, local copies, waits for them, and re-layouts  2.06 us

profile of v1, /device:TPU:0, one launch (start us, length us, event | category | flops | bytes accessed | tf_op | source)
XLA Modules:
  0.0 27.0 jit_solution(13166579655882261710)
XLA Ops:
  0.6 24.3 %shard_map.50 = (f32[3,2,8,256]{3,2,1,0:T(8,128)}, f32[3,2,8,256]{3,2,1,0:T(8,128)}) custom-call(bf16[2,5,2,16,256]{4,3,2,1,0:T(8,128)(2,1)} %adj_hbm.1, bf16[2,5,3,2,16,256]{5,4,3,2,1,0:T(8,128)(2,1)} %flux_hbm.1, f32[2,8,256]{2,1,0:T(8,128)} %shift_hbm.1), custom_call_target="tpu_custom_call" | custom-call | tf_op jit(solution)/shard_map/pallas_call | solution.py:395
  25.0 0.0 copy-start
  25.0 1.4 %copy.7 = f32[3,2,8,256]{3,2,1,0:T(8,128)} copy(f32[3,2,8,256]{3,2,1,0:T(8,128)} %get-tuple-element.4) | data formatting | bytes 98304
  26.4 0.0 copy-done
  26.4 0.6 %copy.8 = f32[3,2,8,256]{3,2,1,0:T(8,128)} copy(f32[3,2,8,256]{3,2,1,0:T(8,128)S(1)} %copy-done) | data formatting | bytes 98304
Async XLA Ops:
  25.0 1.4 %copy-start = (f32[3,2,8,256]{3,2,1,0:T(8,128)S(1)}, f32[3,2,8,256]{3,2,1,0:T(8,128)}, u32[]{:S(2)}) copy-start(f32[3,2,8,256]{3,2,1,0:T(8,128)} %get-tuple-element.5) | copy-start | bytes 147460

commit v2 on v1

--- a/solution.py
+++ b/solution.py
@@ -12,6 +12,7 @@
 CENTER = 10.0
 SPREAD = 8.0
 HALO = 3
+VMEM_GRANT = 24 << 20
 MESH = pl.DeviceIdType.MESH
 F32 = jnp.float32
 
@@ -109,7 +110,7 @@
     adj_hbm, flux_hbm, shift_hbm, x_ref, r_ref,
     adj, flux, halo, part, got, u0, u1, u2, u3, sh, row_out, gath, gath2,
     load_sem, halo_send, halo_recv, sh_send, sh_recv, y_send, y_recv,
-    x_send, x_recv, g_send, g_recv, h_send, h_recv,
+    x_send, x_recv, g_send, g_recv, h_send, h_recv, near,
 ):
     i, c = lax.axis_index("inst"), lax.axis_index("cell")
     wy = window * cols
@@ -129,24 +130,39 @@
     for load in loads:
         load.start()
 
+    def inside(dc):
+        return (c + dc >= 0) & (c + dc < n_cell)
+
     barrier = pltpu.get_barrier_semaphore()
-    for d in range(1, n_cell):
-        pl.semaphore_signal(barrier, inc=1, device_id=(i, lax.rem(c + d, n_cell)), device_id_type=MESH)
+    expected = n_inst - 1
+    for dc in (-1, 1, -2, 2):
+        expected = expected + jnp.where(inside(dc), 1, 0)
+
+        @pl.when(inside(dc))
+        def _():
+            pl.semaphore_signal(barrier, inc=1, device_id=(i, c + dc), device_id_type=MESH)
+
     for d in range(1, n_inst):
         pl.semaphore_signal(barrier, inc=1, device_id=(lax.rem(i + d, n_inst), c), device_id_type=MESH)
-    expected = n_cell - 1 + n_inst - 1
-    for dj in range(-(window - 1), window):
-        if dj == 0:
-            continue
-        for dc in (-1, 1):
-            there = (i + dj >= 0) & (i + dj < n_inst) & (c + dc >= 0) & (c + dc < n_cell)
-            expected = expected + jnp.where(there, 1, 0)
-
-            @pl.when(there)
-            def _():
-                pl.semaphore_signal(barrier, inc=1, device_id=(i + dj, c + dc), device_id_type=MESH)
-
     pl.semaphore_wait(barrier, expected)
+
+    reaches = [r for r in (2, 4, 8, 16, 32, 64) if r < n_cell]
+
+    def hello(number):
+        if number < len(reaches):
+            for dc in (-reaches[number], reaches[number]):
+                @pl.when(inside(dc))
+                def _():
+                    pl.semaphore_signal(
+                        near.at[number], inc=1, device_id=(i, c + dc), device_id_type=MESH
+                    )
+
+    def heard(number):
+        if number < len(reaches):
+            count = 0
+            for dc in (-reaches[number], reaches[number]):
+                count = count + jnp.where(inside(dc), 1, 0)
+            pl.semaphore_wait(near.at[number], count)
 
     def halo_copy(dc):
         side = 0 if dc == 1 else 1
@@ -155,13 +171,11 @@
             halo_send.at[side], halo_recv.at[side], (i, c + dc),
         )
 
-    def inside(dc):
-        return (c + dc >= 0) & (c + dc < n_cell)
-
     for dc in (1, -1):
         @pl.when(inside(dc))
         def _():
             halo_copy(dc).start()
+    hello(0)
 
     def sh_copy(dj, dc):
         j = i + dj
@@ -183,10 +197,14 @@
         for dc in (-1, 0, 1)
         if (dj, dc) != (0, 0)
     ]
-    for dj, dc in sh_moves:
-        @pl.when(sh_valid(dj, dc))
-        def _():
-            sh_copy(dj, dc).start()
+    def sh_start(columns_only):
+        for dj, dc in sh_moves:
+            if (dc == 0) == columns_only:
+                @pl.when(sh_valid(dj, dc))
+                def _():
+                    sh_copy(dj, dc).start()
+
+    sh_start(True)
 
     @pl.when(c == 0)
     def _():
@@ -239,11 +257,17 @@
 
     for k in range(3):
         own_terms(k)
+    heard(0)
+    hello(1)
 
     for dc in (1, -1):
         @pl.when(inside(-dc))
         def _():
             halo_copy(dc).wait_recv()
+
+    sh_start(False)
+    heard(1)
+    hello(2)
 
     def y_copy(k, d):
         j = lax.rem(i + d, n_inst)
@@ -280,6 +304,10 @@
             @pl.when(inside(dc))
             def _():
                 x_copy(k, dc).start()
+
+    for number in range(2, len(reaches)):
+        heard(number)
+        hello(number + 1)
 
     loads[2].wait()
     for dj, dc in sh_moves:
@@ -383,6 +411,17 @@
                 x_copy(k, dc).wait_send()
 
 
+def hand_over(x_in, r_in, x_out, r_out, sem):
+    moves = [
+        pltpu.make_async_copy(x_in, x_out, sem.at[0]),
+        pltpu.make_async_copy(r_in, r_out, sem.at[1]),
+    ]
+    for move in moves:
+        move.start()
+    for move in moves:
+        move.wait()
+
+
 def local(n_inst, n_cell, adjoint, flux_jac, shift):
     rows, cols, nz = shift.shape
     ny = adjoint.shape[3]
@@ -392,10 +431,10 @@
     dma = pltpu.SemaphoreType.DMA
     out = jax.ShapeDtypeStruct((3, rows, cols, nz), F32)
     peers = max(n_inst - 1, 1)
-    return pl.pallas_call(
+    answers = pl.pallas_call(
         functools.partial(kernel, n_inst, n_cell, cols, window),
         out_shape=(out, out),
-        in_specs=[pl.BlockSpec(memory_space=pl.ANY)] * 3,
+        in_specs=[pl.BlockSpec(memory_space=pltpu.HBM)] * 3,
         out_specs=(pl.BlockSpec(memory_space=pltpu.VMEM),) * 2,
         scratch_shapes=[
             pltpu.VMEM(adjoint.shape, adjoint.dtype),
@@ -415,9 +454,20 @@
             dma((4, 3)), dma((4, 3)),
             dma((n_cell - 1,)), dma((n_cell - 1,)),
             dma((peers,)), dma((peers,)),
+            pltpu.SemaphoreType.REGULAR((6,)),
         ],
-        compiler_params=pltpu.CompilerParams(collective_id=0, has_side_effects=True),
-    )(adjoint, flux_jac, shift)
+        compiler_params=pltpu.CompilerParams(
+            collective_id=0, has_side_effects=True, vmem_limit_bytes=VMEM_GRANT
+        ),
+    )(*[pltpu.with_memory_space_constraint(a, pltpu.HBM) for a in (adjoint, flux_jac, shift)])
+    return pl.pallas_call(
+        hand_over,
+        out_shape=(out, out),
+        in_specs=[pl.BlockSpec(memory_space=pltpu.VMEM)] * 2,
+        out_specs=(pl.BlockSpec(memory_space=pltpu.HBM),) * 2,
+        scratch_shapes=[dma((2,))],
+        compiler_params=pltpu.CompilerParams(vmem_limit_bytes=1 << 20),
+    )(*answers)
 
 
 def solution(mesh):

time: 27.2 us -> 24.9 us (0.915)
  local copies, waits for them, and re-layouts: 2.06 us -> 0 us
    unnamed x4 -> x0, local copies, waits for them, and re-layouts: 2.06 us -> none
    pallas_call x1, Pallas kernels: 24.3 us -> 23.5 us  [local(): pl.pallas_call(functools.partial(kernel, n_inst, n_cell, cols, window), o...]
    pallas_call x0 -> x1, Pallas kernels: none -> 0.66 us  [local(): pl.pallas_call(hand_over, out_shape=(out, out), in_specs=[pl.BlockSpec(me...]
where the time goes in v2:
time: 24.9 us; the launch traced here: 24.7 us
  Pallas kernels  24.1 us (97%)
  between operations  0.64 us (3%)
    pallas_call x1, Pallas kernels, local(): pl.pallas_call(functools.partial(kernel, n_inst, n_cell, cols, window), o...  23.5 us
    pallas_call x1, Pallas kernels, local(): pl.pallas_call(hand_over, out_shape=(out, out), in_specs=[pl.BlockSpec(me...  0.66 us

profile of v2, /device:TPU:0, one launch (start us, length us, event | category | flops | bytes accessed | tf_op | source)
XLA Modules:
  0.0 24.7 jit_solution(4489687963372119688)
XLA Ops:
  0.6 23.5 %shard_map.50 = (f32[3,2,8,256]{3,2,1,0:T(8,128)S(1)}, f32[3,2,8,256]{3,2,1,0:T(8,128)S(1)}) custom-call(bf16[2,5,2,16,256]{4,3,2,1,0:T(8,128)(2,1)} %adj_hbm.1, bf16[2,5,3,2,16,256]{5,4,3,2,1,0:T(8,128)(2,1)} %flux_hbm.1, f32[2,8,256]{2,1,0:T(8,128)} %shift_hbm.1), custom_call_target="tpu_custom_call" | custom-call | tf_op jit(solution)/shard_map/pallas_call | solution.py:434
  24.1 0.7 %shard_map.51 = (f32[3,2,8,256]{3,2,1,0:T(8,128)}, f32[3,2,8,256]{3,2,1,0:T(8,128)}) custom-call(f32[3,2,8,256]{3,2,1,0:T(8,128)S(1)} %get-tuple-element.4.x_in, f32[3,2,8,256]{3,2,1,0:T(8,128)S(1)} %get-tuple-element.5.r_in), custom_call_target="tpu_custom_call" | custom-call | tf_op jit(solution)/shard_map/pallas_call | solution.py:463

commit v3 on v2

--- a/solution.py
+++ b/solution.py
@@ -110,12 +110,17 @@
     adj_hbm, flux_hbm, shift_hbm, x_ref, r_ref,
     adj, flux, halo, part, got, u0, u1, u2, u3, sh, row_out, gath, gath2,
     load_sem, halo_send, halo_recv, sh_send, sh_recv, y_send, y_recv,
-    x_send, x_recv, g_send, g_recv, h_send, h_recv, near,
+    x_send, x_recv, g_send, g_recv, h_send, h_recv, near, shx_send, shx_recv,
 ):
     i, c = lax.axis_index("inst"), lax.axis_index("cell")
     wy = window * cols
     nv = adj.shape[0] * adj.shape[1]
     nz = adj.shape[-1]
+
+    halves = 2 if nz % 256 == 0 else 1
+
+    def lanes(h):
+        return slice(h * (nz // halves), (h + 1) * (nz // halves))
 
     def start_of(j):
         return jnp.clip(j - 1, 0, n_inst - window)
@@ -164,17 +169,20 @@
                 count = count + jnp.where(inside(dc), 1, 0)
             pl.semaphore_wait(near.at[number], count)
 
-    def halo_copy(dc):
+    def halo_copy(dc, h):
         side = 0 if dc == 1 else 1
         return remote(
-            adj_hbm.at[:, :, 1 if dc == 1 else 0], halo.at[side],
-            halo_send.at[side], halo_recv.at[side], (i, c + dc),
+            adj.at[:, :, 1 if dc == 1 else 0, :, lanes(h)], halo.at[side, :, :, :, lanes(h)],
+            halo_send.at[side, h], halo_recv.at[side, h], (i, c + dc),
         )
 
-    for dc in (1, -1):
-        @pl.when(inside(dc))
-        def _():
-            halo_copy(dc).start()
+    loads[0].wait()
+
+    for h in range(halves):
+        for dc in (1, -1):
+            @pl.when(inside(dc))
+            def _():
+                halo_copy(dc, h).start()
     hello(0)
 
     def sh_copy(dj, dc):
@@ -191,20 +199,32 @@
         first = start_of(j)
         return (j >= 0) & (j < n_inst) & inside(dc) & (i >= first) & (i < first + window)
 
-    sh_moves = [
-        (dj, dc)
-        for dj in range(-(window - 1), window)
-        for dc in (-1, 0, 1)
-        if (dj, dc) != (0, 0)
-    ]
-    def sh_start(columns_only):
-        for dj, dc in sh_moves:
-            if (dc == 0) == columns_only:
-                @pl.when(sh_valid(dj, dc))
-                def _():
-                    sh_copy(dj, dc).start()
-
-    sh_start(True)
+    sh_moves = [(dj, 0) for dj in range(-(window - 1), window) if dj != 0]
+    for dj, dc in sh_moves:
+        @pl.when(sh_valid(dj, dc))
+        def _():
+            sh_copy(dj, dc).start()
+
+    def sh_rows_copy(dc):
+        side = 0 if dc == 1 else 1
+        return remote(
+            sh.at[2:4], sh.at[pl.ds(2 - 2 * dc, 2)],
+            shx_send.at[side], shx_recv.at[side], (i, c + dc),
+        )
+
+    def shift_rows():
+        loads[2].wait()
+        for slot in range(window):
+            @pl.when(start_of(i) + slot != i)
+            def _():
+                remote(
+                    shift_hbm, sh.at[2:4, pl.ds(slot * cols, cols)],
+                    sh_send.at[0, 0], sh_recv.at[slot, 1], (i, c),
+                ).wait_recv()
+        for dc in (1, -1):
+            @pl.when(inside(dc))
+            def _():
+                sh_rows_copy(dc).start()
 
     @pl.when(c == 0)
     def _():
@@ -226,7 +246,6 @@
     def _():
         u0[:, 7:8] = jnp.zeros_like(u0[:, 7:8])
 
-    loads[0].wait()
     loads[1].wait()
 
     n_v = adj.shape[1]
@@ -244,96 +263,89 @@
             part[k, 0, ys] = low
             part[k, 1, ys] = -high
 
-    def halo_terms(k):
+    def halo_terms(k, h):
+        ls = lanes(h)
         for y0 in range(0, adj.shape[3], 16):
             ys = slice(y0, y0 + 16)
-            low, high = part[k, 0, ys], part[k, 1, ys]
+            low, high = part[k, 0, ys, ls], part[k, 1, ys, ls]
             for v in range(nv):
                 a, b = v // n_v, v % n_v
-                low = low - flux[a, b, k, 0, ys].astype(F32) * halo[0, a, b, ys].astype(F32)
-                high = high + flux[a, b, k, 1, ys].astype(F32) * halo[1, a, b, ys].astype(F32)
-            part[k, 0, ys] = low
-            part[k, 1, ys] = high
+                f0, f1 = flux[a, b, k, 0, ys, ls], flux[a, b, k, 1, ys, ls]
+                low = low - f0.astype(F32) * halo[0, a, b, ys, ls].astype(F32)
+                high = high + f1.astype(F32) * halo[1, a, b, ys, ls].astype(F32)
+            part[k, 0, ys, ls] = low
+            part[k, 1, ys, ls] = high
 
     for k in range(3):
         own_terms(k)
     heard(0)
     hello(1)
 
-    for dc in (1, -1):
-        @pl.when(inside(-dc))
-        def _():
-            halo_copy(dc).wait_recv()
-
-    sh_start(False)
-    heard(1)
-    hello(2)
-
-    def y_copy(k, d):
+    def y_copy(k, d, h):
         j = lax.rem(i + d, n_inst)
         at = pl.multiple_of(start_of(j) * cols, cols)
         return remote(
-            part.at[k, :, pl.ds(at, wy)], got.at[d - 1, k],
-            y_send.at[d - 1, k], y_recv.at[d - 1, k], (j, c),
+            part.at[k, :, pl.ds(at, wy), lanes(h)], got.at[d - 1, k, :, :, lanes(h)],
+            y_send.at[d - 1, k, h], y_recv.at[d - 1, k, h], (j, c),
         )
 
-    for k in range(3):
-        halo_terms(k)
-        for d in range(1, n_inst):
-            y_copy(k, d).start()
+    for h in range(halves):
+        for dc in (1, -1):
+            @pl.when(inside(-dc))
+            def _():
+                halo_copy(dc, h).wait_recv()
+        for k in range(3):
+            halo_terms(k, h)
+            for d in range(1, n_inst):
+                y_copy(k, d, h).start()
+        if h == 0:
+            shift_rows()
+    heard(1)
+    hello(2)
 
     x_moves = {1: (3, 1, 2), -1: (3, 5, 2), 2: (4, 0, 1), -2: (3, 7, 1)}
 
-    def x_copy(k, dc):
+    def x_copy(k, dc, h):
         src, dst, rows = x_moves[dc]
         slot = sorted(x_moves).index(dc)
         return remote(
-            u0.at[k, pl.ds(src, rows)], u0.at[k, pl.ds(dst, rows)],
-            x_send.at[slot, k], x_recv.at[slot, k], (i, c + dc),
+            u0.at[k, pl.ds(src, rows), :, lanes(h)], u0.at[k, pl.ds(dst, rows), :, lanes(h)],
+            x_send.at[slot, k, h], x_recv.at[slot, k, h], (i, c + dc),
         )
 
     my_at = pl.multiple_of(start_of(i) * cols, cols)
-    for k in range(3):
-        for d in range(1, n_inst):
-            y_copy(k, d).wait_recv()
-        total = part[k, :, pl.ds(my_at, wy)]
-        for d in range(1, n_inst):
-            total = total + got[d - 1, k]
-        u0[k, 3:5] = total
-        for dc in x_moves:
-            @pl.when(inside(dc))
-            def _():
-                x_copy(k, dc).start()
+    for h in range(halves):
+        for k in range(3):
+            for d in range(1, n_inst):
+                y_copy(k, d, h).wait_recv()
+            total = part[k, :, pl.ds(my_at, wy), lanes(h)]
+            for d in range(1, n_inst):
+                total = total + got[d - 1, k, :, :, lanes(h)]
+            u0[k, 3:5, :, lanes(h)] = total
+            for dc in x_moves:
+                @pl.when(inside(dc))
+                def _():
+                    x_copy(k, dc, h).start()
 
     for number in range(2, len(reaches)):
         heard(number)
         hello(number + 1)
 
-    loads[2].wait()
     for dj, dc in sh_moves:
         @pl.when(sh_valid(dj, dc))
         def _():
             sh_copy(dj, dc).wait_send()
-    for slot in range(window):
-        for dc in (-1, 0, 1):
-            owner = start_of(i) + slot
-            there = inside(-dc)
-            if dc == 0:
-                there = there & (owner != i)
-
-            @pl.when(there)
-            def _():
-                at = slot * cols
-                remote(
-                    shift_hbm, sh.at[pl.ds(2 - 2 * dc, 2), pl.ds(at, cols)],
-                    sh_send.at[0, 0], sh_recv.at[slot, dc + 1], (i, c),
-                ).wait_recv()
-
-    for k in range(3):
-        for dc in x_moves:
-            @pl.when(inside(-dc))
-            def _():
-                x_copy(k, dc).wait_recv()
+    for dc in (1, -1):
+        @pl.when(inside(-dc))
+        def _():
+            sh_rows_copy(dc).wait_recv()
+
+    for h in range(halves):
+        for k in range(3):
+            for dc in x_moves:
+                @pl.when(inside(-dc))
+                def _():
+                    x_copy(k, dc, h).wait_recv()
 
     shape = (wy, nz)
     y_at = lax.broadcasted_iota(jnp.int32, shape, 0)
@@ -401,14 +413,19 @@
     for dc in (1, -1):
         @pl.when(inside(dc))
         def _():
-            halo_copy(dc).wait_send()
-    for k in range(3):
-        for d in range(1, n_inst):
-            y_copy(k, d).wait_send()
-        for dc in x_moves:
+            sh_rows_copy(dc).wait_send()
+    for h in range(halves):
+        for dc in (1, -1):
             @pl.when(inside(dc))
             def _():
-                x_copy(k, dc).wait_send()
+                halo_copy(dc, h).wait_send()
+        for k in range(3):
+            for d in range(1, n_inst):
+                y_copy(k, d, h).wait_send()
+            for dc in x_moves:
+                @pl.when(inside(dc))
+                def _():
+                    x_copy(k, dc, h).wait_send()
 
 
 def hand_over(x_in, r_in, x_out, r_out, sem):
@@ -448,13 +465,14 @@
             pltpu.VMEM((n_cell - 1, 1, 128), F32),
             pltpu.VMEM((peers, 1, 128), F32),
             dma((3,)),
-            dma((2,)), dma((2,)),
+            dma((2, 2)), dma((2, 2)),
             dma((2 * window - 1, 3)), dma((window, 3)),
-            dma((peers, 3)), dma((peers, 3)),
-            dma((4, 3)), dma((4, 3)),
+            dma((peers, 3, 2)), dma((peers, 3, 2)),
+            dma((4, 3, 2)), dma((4, 3, 2)),
             dma((n_cell - 1,)), dma((n_cell - 1,)),
             dma((peers,)), dma((peers,)),
             pltpu.SemaphoreType.REGULAR((6,)),
+            dma((2,)), dma((2,)),
         ],
         compiler_params=pltpu.CompilerParams(
             collective_id=0, has_side_effects=True, vmem_limit_bytes=VMEM_GRANT

time: 24.9 us -> 23.6 us (0.948)
  Pallas kernels: 24.1 us -> 22.8 us
    pallas_call x1, Pallas kernels: 23.5 us -> 22.1 us  [local(): pl.pallas_call(functools.partial(kernel, n_inst, n_cell, cols, window), o...]
where the time goes in v3:
time: 23.6 us; the launch traced here: 23.4 us
  Pallas kernels  22.8 us (97%)
  between operations  0.64 us (3%)
    pallas_call x1, Pallas kernels, local(): pl.pallas_call(functools.partial(kernel, n_inst, n_cell, cols, window), o...  22.1 us
    pallas_call x1, Pallas kernels, local(): pl.pallas_call(hand_over, out_shape=(out, out), in_specs=[pl.BlockSpec(me...  0.66 us

profile of v3, /device:TPU:0, one launch (start us, length us, event | category | flops | bytes accessed | tf_op | source)
XLA Modules:
  0.0 23.4 jit_solution(2208140733766374052)
XLA Ops:
  0.6 22.1 %shard_map.50 = (f32[3,2,8,256]{3,2,1,0:T(8,128)S(1)}, f32[3,2,8,256]{3,2,1,0:T(8,128)S(1)}) custom-call(bf16[2,5,2,16,256]{4,3,2,1,0:T(8,128)(2,1)} %adj_hbm.1, bf16[2,5,3,2,16,256]{5,4,3,2,1,0:T(8,128)(2,1)} %flux_hbm.1, f32[2,8,256]{2,1,0:T(8,128)} %shift_hbm.1), custom_call_target="tpu_custom_call" | custom-call | tf_op jit(solution)/shard_map/pallas_call | solution.py:451
  22.8 0.7 %shard_map.51 = (f32[3,2,8,256]{3,2,1,0:T(8,128)}, f32[3,2,8,256]{3,2,1,0:T(8,128)}) custom-call(f32[3,2,8,256]{3,2,1,0:T(8,128)S(1)} %get-tuple-element.4.x_in, f32[3,2,8,256]{3,2,1,0:T(8,128)S(1)} %get-tuple-element.5.r_in), custom_call_target="tpu_custom_call" | custom-call | tf_op jit(solution)/shard_map/pallas_call | solution.py:481

commit v4 on v3

--- a/solution.py
+++ b/solution.py
@@ -61,6 +61,28 @@
                 out = (diag * u - beside + LAME * (shifted[k] - dv)) * (1.0 / SPREAD)
                 dst[k, row] = jnp.where(valid_row(row), out, 0.0)
         before = dv
+
+
+def energy(src, sh, edges):
+    _, y_last, _, z_last = edges
+    wy, nz = src.shape[2], src.shape[3]
+    total = None
+    for row in (3, 4):
+        dv = None
+        for k in range(3):
+            v = src[k, row]
+            above = (
+                src[k, row + 1],
+                jnp.where(y_last, 0.0, pltpu.roll(v, wy - 1, 0)),
+                jnp.where(z_last, 0.0, pltpu.roll(v, nz - 1, 1)),
+            )
+            step = above[k] - v
+            dv = step if dv is None else dv + step
+            diag = sh[row - 1] + (6.0 - CENTER)
+            term = v * (diag * v - 2.0 * (above[0] + above[1] + above[2]))
+            total = term if total is None else total + term
+        total = total + LAME * (dv * dv)
+    return total * (1.0 / SPREAD)
 
 
 def coefficients(mu):
@@ -322,7 +344,7 @@
             for d in range(1, n_inst):
                 total = total + got[d - 1, k, :, :, lanes(h)]
             u0[k, 3:5, :, lanes(h)] = total
-            for dc in x_moves:
+            for dc in (1, -1, -2):
                 @pl.when(inside(dc))
                 def _():
                     x_copy(k, dc, h).start()
@@ -340,12 +362,15 @@
         def _():
             sh_rows_copy(dc).wait_recv()
 
-    for h in range(halves):
-        for k in range(3):
-            for dc in x_moves:
-                @pl.when(inside(-dc))
-                def _():
-                    x_copy(k, dc, h).wait_recv()
+    def field_arrived(directions):
+        for h in range(halves):
+            for k in range(3):
+                for dc in directions:
+                    @pl.when(inside(-dc))
+                    def _():
+                        x_copy(k, dc, h).wait_recv()
+
+    field_arrived((1, -1, -2))
 
     shape = (wy, nz)
     y_at = lax.broadcasted_iota(jnp.int32, shape, 0)
@@ -356,17 +381,28 @@
         place = 2 * c + row - HALO
         return (place >= 0) & (place < 2 * n_cell)
 
-    apply_operator(u0, u1, sh, 1, 6, valid_row, edges)
-    apply_operator(u1, u2, sh, 2, 5, valid_row, edges)
-    apply_operator(u2, u3, sh, 3, 4, valid_row, edges)
+    apply_operator(u0, u1, sh, 2, 6, valid_row, edges)
+    apply_operator(u1, u2, sh, 3, 5, valid_row, edges)
+
+    def rest():
+        for h in range(halves):
+            for k in range(3):
+                @pl.when(inside(2))
+                def _():
+                    x_copy(k, 2, h).start()
+
+        field_arrived((2,))
+        apply_operator(u0, u1, sh, 1, 1, valid_row, edges)
+        apply_operator(u1, u2, sh, 2, 2, valid_row, edges)
+        apply_operator(u2, u3, sh, 3, 4, valid_row, edges)
 
     basis = (u0, u1, u2, u3)
     lane = lax.broadcasted_iota(jnp.int32, (1, 128), 1)
     packed = jnp.zeros((1, 128), F32)
     for m in range(6):
+        total = energy(u2, sh, edges) if m == 5 else None
         a, b = basis[m // 2], basis[(m + 1) // 2]
-        total = None
-        for k in range(3):
+        for k in range(3 if m < 5 else 0):
             for row in (3, 4):
                 term = a[k, row] * b[k, row]
                 total = term if total is None else total + term
@@ -375,7 +411,7 @@
         value = jnp.sum(jnp.sum(total, axis=0, keepdims=True), axis=1, keepdims=True)
         packed = jnp.where(lane == m, value, packed)
 
-    def gather_sum(packed, slot, buffer, send, recv, count, device):
+    def gather_sum(packed, slot, buffer, send, recv, count, device, meanwhile):
         row_out[slot] = packed
         moves = [
             remote(row_out.at[slot], buffer.at[d - 1], send.at[d - 1], recv.at[d - 1], device(d))
@@ -383,6 +419,7 @@
         ]
         for move in moves:
             move.start()
+        meanwhile()
         total = packed
         for d, move in enumerate(moves):
             move.wait_recv()
@@ -392,11 +429,12 @@
         return total
 
     packed = gather_sum(
-        packed, 0, gath, g_send, g_recv, n_cell, lambda d: (i, lax.rem(c + d, n_cell))
+        packed, 0, gath, g_send, g_recv, n_cell, lambda d: (i, lax.rem(c + d, n_cell)), rest
     )
     if window < n_inst:
         packed = gather_sum(
-            packed, 1, gath2, h_send, h_recv, n_inst, lambda d: (lax.rem(i + d, n_inst), c)
+            packed, 1, gath2, h_send, h_recv, n_inst, lambda d: (lax.rem(i + d, n_inst), c),
+            lambda: None,
         )
     mu = [
         jnp.sum(jnp.where(lane == m, packed, 0.0), axis=1, keepdims=True) for m in range(6)

time: 23.6 us -> 22.9 us (0.970)
  Pallas kernels: 22.8 us -> 22.2 us
    pallas_call x1, Pallas kernels: 22.1 us -> 21.5 us  [local(): pl.pallas_call(functools.partial(kernel, n_inst, n_cell, cols, window), o...]
where the time goes in v4:
time: 22.9 us; the launch traced here: 22.8 us
  Pallas kernels  22.2 us (97%)
  between operations  0.64 us (3%)
    pallas_call x1, Pallas kernels, local(): pl.pallas_call(functools.partial(kernel, n_inst, n_cell, cols, window), o...  21.5 us
    pallas_call x1, Pallas kernels, local(): pl.pallas_call(hand_over, out_shape=(out, out), in_specs=[pl.BlockSpec(me...  0.66 us

profile of v4, /device:TPU:0, one launch (start us, length us, event | category | flops | bytes accessed | tf_op | source)
XLA Modules:
  0.0 22.8 jit_solution(13398534297123288804)
XLA Ops:
  0.6 21.5 %shard_map.50 = (f32[3,2,8,256]{3,2,1,0:T(8,128)S(1)}, f32[3,2,8,256]{3,2,1,0:T(8,128)S(1)}) custom-call(bf16[2,5,2,16,256]{4,3,2,1,0:T(8,128)(2,1)} %adj_hbm.1, bf16[2,5,3,2,16,256]{5,4,3,2,1,0:T(8,128)(2,1)} %flux_hbm.1, f32[2,8,256]{2,1,0:T(8,128)} %shift_hbm.1), custom_call_target="tpu_custom_call" | custom-call | tf_op jit(solution)/shard_map/pallas_call | solution.py:489
  22.1 0.7 %shard_map.51 = (f32[3,2,8,256]{3,2,1,0:T(8,128)}, f32[3,2,8,256]{3,2,1,0:T(8,128)}) custom-call(f32[3,2,8,256]{3,2,1,0:T(8,128)S(1)} %get-tuple-element.4.x_in, f32[3,2,8,256]{3,2,1,0:T(8,128)S(1)} %get-tuple-element.5.r_in), custom_call_target="tpu_custom_call" | custom-call | tf_op jit(solution)/shard_map/pallas_call | solution.py:519
